TPU v7x, 32 devices: a whole 2x2x4 slice. The times are simulated.
32 devices in a mesh: sample: 4 (over x, core), space: 8 (over z, y).
Axes of the slice: x: 2, y: 2, z: 4, core: 2. Of those that a mesh axis runs over, the one named last changes fastest.
Arguments:
- acts: bfloat16 [8, 8, 16, 8, 8, 128], P('sample', 'space'), may hold values from -6 to 6
- weight: float32 [3456, 128], P('space'), may hold values from -0.109375 to 0.109375
- moment: float32 [3456, 128], P('space'), may hold values from -3 to 3
- second: float32 [3456, 128], P('space'), may hold values from 0.05 to 2
- cotangent: bfloat16 [8, 8, 16, 8, 8, 128], P('sample', 'space'), may hold values from -6 to 6
Outputs:
- output: bfloat16 [8, 8, 16, 8, 8, 128], P('sample', 'space')
- input_grad: bfloat16 [8, 8, 16, 8, 8, 128], P('sample', 'space')
- weight_grad: float32 [3456, 128], P('space')
- new_weight: float32 [3456, 128], P('space')
- new_moment: float32 [3456, 128], P('space')
- new_second: float32 [3456, 128], P('space')
All inputs are finite; a program needn't handle non-finite values.
Results may differ from a plain program's by a relative error of at most 0.0062.
Values may be sent and summed in bfloat16 or wider, within the bound.
A program may use at most 64 MiB of HBM per device.

v0:
```python
import jax
import jax.numpy as jnp
from jax import lax
from jax.sharding import PartitionSpec as P

GY = 2
GZ = 4
root_coef = 0.7978845608
cubic_coef = 0.044715


def shifted(value, axis, by):
    devices = lax.axis_size(axis)
    pairs = [(i, i + by) for i in range(devices) if 0 <= i + by < devices]
    return lax.ppermute(value, axis, pairs)


def convolve(field, kernel):
    return lax.conv_general_dilated(
        field,
        kernel,
        (1, 1, 1),
        "VALID",
        dimension_numbers=("NDHWC", "DHWIO", "NDHWC"),
        preferred_element_type=jnp.float32,
    )


def activate(pre):
    inner = root_coef * (pre + cubic_coef * pre * pre * pre)
    tval = jnp.tanh(inner)
    value = 0.5 * pre * (1.0 + tval)
    slope = 0.5 * (1.0 + tval) + 0.5 * pre * (1.0 - tval * tval) * root_coef * (
        1.0 + 3.0 * cubic_coef * pre * pre
    )
    return (value, slope)


def extend(field):
    place = lax.axis_index("space")
    groups = lax.axis_size("space") // (GY * GZ)
    coord_z = place % GZ
    coord_y = place // GZ % GY
    coord_x = place // (GZ * GY)
    for dim, stride, coord, count in (
        (3, 1, coord_z, GZ),
        (2, GZ, coord_y, GY),
        (1, GY * GZ, coord_x, groups),
    ):
        length = field.shape[dim]
        first_layer = lax.slice_in_dim(field, 0, 1, 1, dim)
        last_layer = lax.slice_in_dim(field, length - 1, length, 1, dim)
        below = shifted(last_layer, "space", stride)
        above = shifted(first_layer, "space", -stride)
        below = jnp.where(coord > 0, below, jnp.zeros_like(below))
        above = jnp.where(coord < count - 1, above, jnp.zeros_like(above))
        field = jnp.concatenate([below, field, above], dim)
    return field


def kernel_terms(padded, grad_pre):
    nx, ny, nz = (grad_pre.shape[1], grad_pre.shape[2], grad_pre.shape[3])
    terms = []
    for kx in range(3):
        for ky in range(3):
            for kz in range(3):
                window = padded[:, kx : kx + nx, ky : ky + ny, kz : kz + nz, :]
                terms.append(
                    lax.dot_general(
                        window,
                        grad_pre,
                        (((0, 1, 2, 3), (0, 1, 2, 3)), ((), ())),
                        preferred_element_type=jnp.float32,
                    )
                )
    stacked = jnp.stack(terms, 0)
    return stacked.reshape(27 * stacked.shape[1], stacked.shape[2])


def local(acts, weight, moment, second, cotangent):
    field = acts[:, 0]
    grad_out = cotangent[:, 0]
    channels = weight.shape[1]
    rows_bf = weight.astype(jnp.bfloat16)
    whole = lax.all_gather(rows_bf, "space", axis=0, tiled=True)
    kernel = whole.reshape(3, 3, 3, channels, channels)
    padded = extend(field)
    pre = convolve(padded, kernel)
    value, slope = activate(pre)
    output = value.astype(jnp.bfloat16)
    grad_pre = (grad_out.astype(jnp.float32) * slope).astype(jnp.bfloat16)
    flipped = jnp.flip(kernel, (0, 1, 2)).transpose(0, 1, 2, 4, 3)
    grad_padded = extend(grad_pre)
    input_grad = convolve(grad_padded, flipped).astype(jnp.bfloat16)
    total = (
        field.shape[0]
        * lax.axis_size("sample")
        * lax.axis_size("space")
        * field.shape[1]
        * field.shape[2]
        * field.shape[3]
    )
    local_terms = kernel_terms(padded, grad_pre) * float(total) ** (-0.5)
    owned = lax.psum_scatter(local_terms, "space", scatter_dimension=0, tiled=True)
    weight_grad = lax.psum(owned, "sample")
    new_moment = 0.9 * moment + 0.1 * weight_grad
    new_second = 0.999 * second + 0.001 * weight_grad * weight_grad
    first_fix = 1.0 - 0.9**10
    second_fix = 1.0 - 0.999**10
    new_weight = weight - 0.001 * (new_moment / first_fix) / (
        jnp.sqrt(new_second / second_fix) + 1e-08
    )
    return (output[:, None], input_grad[:, None], weight_grad, new_weight, new_moment, new_second)


def solution(mesh):
    in_specs = (
        P("sample", "space", None, None, None, None),
        P("space", None),
        P("space", None),
        P("space", None),
        P("sample", "space", None, None, None, None),
    )
    out_specs = (
        P("sample", "space", None, None, None, None),
        P("sample", "space", None, None, None, None),
        P("space", None),
        P("space", None),
        P("space", None),
        P("space", None),
    )
    return jax.shard_map(local, mesh=mesh, in_specs=in_specs, out_specs=out_specs, check_vma=False)
```

profile of v0, /device:TPU:0, one launch (start us, length us, event | category | flops | bytes accessed | tf_op | source)
XLA Modules:
  0.0 203.3 jit_solution(16130695142617238557)
XLA Ops:
  7.2 1.5 fusion.71
  8.7 1.3 collective-permute-start.1
  10.0 5.5 %collective-permute-start = (bf16[2,16,8,1,128]{4,3,2,1,0:T(2,128)(2,1)S(1)}, bf16[2,16,8,1,128]{4,3,2,1,0:T(2,128)(2,1)S(1)}, u32[]{:S(2)}, u32[]{:S(2)}) collective-permute-start(bf16[2,16,8,1,128]{4,3,2,1,0:T(2,128)(2,1)S(1)} %get-tuple-element.37), channel_id=1, source_target_pairs={{0,1},{1,2},{2,3},{3,4},{4,5},{5,6},{6,7},{8,9},{9,10},{10,11},{11... | collective-permute-start | bytes 196616 | tf_op jit(solution)/shard_map/ppermute | solution.py:15
  15.5 1.0 convert_element_type.18
  16.5 0.6 collective-permute-done.1
  17.2 2.8 %collective-permute-done = bf16[2,16,8,1,128]{4,3,2,1,0:T(2,128)(2,1)S(1)} collective-permute-done((bf16[2,16,8,1,128]{4,3,2,1,0:T(2,128)(2,1)S(1)}, bf16[2,16,8,1,128]{4,3,2,1,0:T(2,128)(2,1)S(1)}, u32[]{:S(2)}, u32[]{:S(2)}) %collective-permute-start) | collective-permute-done | bytes 65568 | tf_op jit(solution)/shard_map/ppermute | solution.py:15
  20.4 1.3 collective-permute-start.3
  21.7 35.9 %all_gather.3 = bf16[3456,128]{1,0:T(8,128)(2,1)S(1)} all-gather(bf16[432,128]{1,0:T(8,128)(2,1)S(1)} %convert_element_type.18), channel_id=1, replica_groups=mesh['sample'=4,'space'=8] {'space'}, dimensions={0}, use_global_device_ids=true | all-gather | bytes 995328 | tf_op jit(solution)/shard_map/all_gather | solution.py:85
  57.6 1.3 collective-permute-start.2
  58.9 2.5 %collective-permute-done.2 = bf16[2,16,1,10,128]{4,3,2,1,0:T(8,128)(2,1)S(1)} collective-permute-done((bf16[2,16,1,10,128]{4,3,2,1,0:T(8,128)(2,1)S(1)}, bf16[2,16,1,10,128]{4,3,2,1,0:T(8,128)(2,1)S(1)}, u32[]{:S(2)}, u32[]{:S(2)}) %collective-permute-start.2) | collective-permute-done | bytes 81952 | tf_op jit(solution)/shard_map/ppermute | solution.py:15
  61.5 0.7 collective-permute-start.5
  62.1 1.4 pad_maximum_fusion.3
  63.5 0.7 collective-permute-start.4
  64.2 0.7 pad_maximum_fusion
  65.0 1.5 pad_maximum_fusion.2
  66.6 6.3 %fusion.36 = f32[2,16,8,8,128]{4,0,3,2,1:T(2,128)S(1)} fusion(bf16[3,3,3,128,128]{4,3,2,1,0:T(8,128)(2,1)S(1)} %bitcast.272, bf16[2,18,10,10,128]{4,3,2,1,0:T(8,128)(2,1)S(1)} %pad_maximum_fusion), kind=kOutput, calls=%fused_computation.73 | convolution fusion | flops 1811939328 | bytes 2854912 | tf_op jit(solution)/shard_map/conv_general_dilated | solution.py:19
  72.9 1.6 fusion.34
  74.8 0.4 fusion.26
  75.2 0.4 fusion.25
  77.0 0.4 fusion.20
  77.4 0.4 fusion.19
  78.1 0.4 fusion.17
  78.5 0.4 fusion.16
  78.9 0.4 fusion.15
  79.7 0.5 fusion.13
  81.6 0.4 fusion.8
  82.0 0.4 fusion.7
  82.7 0.4 fusion.5
  83.1 0.4 fusion.4
  83.9 0.4 fusion.2
  84.2 0.4 fusion.1
  84.6 1.4 broadcast_multiply_fusion
  86.3 1.3 collective-permute-start.7
  87.6 4.6 %collective-permute-start.6 = (bf16[2,16,8,1,128]{4,3,2,1,0:T(2,128)(2,1)S(1)}, bf16[2,16,8,1,128]{4,3,2,1,0:T(2,128)(2,1)S(1)}, u32[]{:S(2)}, u32[]{:S(2)}) collective-permute-start(bf16[2,16,8,1,128]{4,3,2,1,0:T(2,128)(2,1)S(1)} %get-tuple-element.35), channel_id=1, source_target_pairs={{0,1},{1,2},{2,3},{3,4},{4,5},{5,6},{6,7},{8,9},{9,10},{10,11},{11... | collective-permute-start | bytes 196616 | tf_op jit(solution)/shard_map/ppermute | solution.py:15
  92.2 1.0 collective-permute-done.7
  93.3 1.3 collective-permute-done.6
  95.0 1.3 collective-permute-start.9
  96.3 18.0 %collective-permute-start.8 = (bf16[2,16,1,10,128]{4,3,2,1,0:T(8,128)(2,1)S(1)}, bf16[2,16,1,10,128]{4,3,2,1,0:T(8,128)(2,1)S(1)}, u32[]{:S(2)}, u32[]{:S(2)}) collective-permute-start(bf16[2,16,1,10,128]{4,3,2,1,0:T(8,128)(2,1)S(1)} %get-tuple-element.31), channel_id=1, source_target_pairs={{0,4},{1,5},{2,6},{3,7},{8,12},{9,13},{10,14},{11,15},{16,20},{17,... | collective-permute-start | bytes 245768 | tf_op jit(solution)/shard_map/ppermute | solution.py:15
  114.3 3.2 %collective-permute-done.9 = bf16[2,16,1,10,128]{4,3,2,1,0:T(8,128)(2,1)S(1)} collective-permute-done((bf16[2,16,1,10,128]{4,3,2,1,0:T(8,128)(2,1)S(1)}, bf16[2,16,1,10,128]{4,3,2,1,0:T(8,128)(2,1)S(1)}, u32[]{:S(2)}, u32[]{:S(2)}) %collective-permute-start.9) | collective-permute-done | bytes 81952 | tf_op jit(solution)/shard_map/ppermute | solution.py:15
  117.9 0.7 collective-permute-start.11
  118.5 0.9 collective-permute-start.10
  119.5 0.7 pad_maximum_fusion.1
  120.2 39.6 %reduce-scatter.2.cloned.1.call-done = f32[432,128]{1,0:T(8,128)} async-done(((f32[3456,128]{1,0:T(8,128)}), f32[432,128]{1,0:T(8,128)}) %reduce-scatter.2.cloned.1.call-update) | async-done | bytes 221200 | tf_op jit(solution)/shard_map/reduce_scatter | solution.py:104
  159.9 7.3 %fusion = bf16[2,1,16,8,8,128]{5,0,4,3,2,1:T(2,128)(2,1)S(1)} fusion(bf16[3,3,3,128,128]{4,3,2,1,0:T(8,128)(2,1)} %bitcast.273, bf16[2,18,10,10,128]{4,3,2,1,0:T(8,128)(2,1)S(1)} %pad_maximum_fusion.1), kind=kOutput, calls=%fused_computation.7 | convolution fusion | flops 1812201472 | bytes 2330624 | tf_op jit(solution)/shard_map/conv_general_dilated | solution.py:19
  167.2 0.9 copy.134
  168.1 24.8 %all-reduce.2.cloned.1.call-done = f32[432,128]{1,0:T(8,128)} async-done(((f32[432,128]{1,0:T(8,128)}), f32[432,128]{1,0:T(8,128)}) %all-reduce.2.cloned.1.call-update) | async-done | bytes 221200 | tf_op jit(solution)/shard_map/psum | solution.py:105
  192.9 1.8 divide_subtract_fusion
  194.8 1.6 copy.256
  (52 shorter events, 6.4 us)
Async XLA Ops:
  7.2 13.0 %copy-start = (bf16[2,1,16,8,8,128]{5,4,3,2,1,0:T(8,128)(2,1)S(1)}, bf16[2,1,16,8,8,128]{5,4,3,2,1,0:T(8,128)(2,1)}, u32[]{:S(2)}) copy-start(bf16[2,1,16,8,8,128]{5,4,3,2,1,0:T(8,128)(2,1)} %param.5) | copy-start | bytes 1572868
  7.2 152.7 %reduce-scatter.2.cloned.1.call-start = ((), (), s32[]{:S(2)}) async-start(), calls=%async_computation.1 | async-start | bytes 1990656 | tf_op jit(solution)/shard_map/reduce_scatter | solution.py:104
  8.7 8.4 %collective-permute-start.1 = (bf16[2,16,8,1,128]{4,3,2,1,0:T(2,128)(2,1)S(1)}, bf16[2,16,8,1,128]{4,3,2,1,0:T(2,128)(2,1)S(1)}, u32[]{:S(2)}, u32[]{:S(2)}) collective-permute-start(bf16[2,16,8,1,128]{4,3,2,1,0:T(2,128)(2,1)S(1)} %get-tuple-element.38), channel_id=1, source_target_pairs={{1,0},{2,1},{3,2},{4,3},{5,4},{6,5},{7,6},{9,8},{10,9},{11,10},{12... | collective-permute-start | bytes 196616 | tf_op jit(solution)/shard_map/ppermute | solution.py:15
  10.0 10.1 %collective-permute-start = (bf16[2,16,8,1,128]{4,3,2,1,0:T(2,128)(2,1)S(1)}, bf16[2,16,8,1,128]{4,3,2,1,0:T(2,128)(2,1)S(1)}, u32[]{:S(2)}, u32[]{:S(2)}) collective-permute-start(bf16[2,16,8,1,128]{4,3,2,1,0:T(2,128)(2,1)S(1)} %get-tuple-element.37), channel_id=1, source_target_pairs={{0,1},{1,2},{2,3},{3,4},{4,5},{5,6},{6,7},{8,9},{9,10},{10,11},{11... | collective-permute-start | bytes 196616 | tf_op jit(solution)/shard_map/ppermute | solution.py:15
  20.4 38.5 %collective-permute-start.3 = (bf16[2,16,1,10,128]{4,3,2,1,0:T(8,128)(2,1)S(1)}, bf16[2,16,1,10,128]{4,3,2,1,0:T(8,128)(2,1)S(1)}, u32[]{:S(2)}, u32[]{:S(2)}) collective-permute-start(bf16[2,16,1,10,128]{4,3,2,1,0:T(8,128)(2,1)S(1)} %get-tuple-element.34), channel_id=1, source_target_pairs={{4,0},{5,1},{6,2},{7,3},{12,8},{13,9},{14,10},{15,11},{20,16},{21,... | collective-permute-start | bytes 245768 | tf_op jit(solution)/shard_map/ppermute | solution.py:15
  57.6 9.0 %copy-start.2 = (bf16[3456,128]{1,0:T(8,128)(2,1)}, bf16[3456,128]{1,0:T(8,128)(2,1)S(1)}, u32[]{:S(2)}) copy-start(bf16[3456,128]{1,0:T(8,128)(2,1)S(1)} %all_gather.3) | copy-start | bytes 2654212
  57.6 3.8 %collective-permute-start.2 = (bf16[2,16,1,10,128]{4,3,2,1,0:T(8,128)(2,1)S(1)}, bf16[2,16,1,10,128]{4,3,2,1,0:T(8,128)(2,1)S(1)}, u32[]{:S(2)}, u32[]{:S(2)}) collective-permute-start(bf16[2,16,1,10,128]{4,3,2,1,0:T(8,128)(2,1)S(1)} %get-tuple-element.33), channel_id=1, source_target_pairs={{0,4},{1,5},{2,6},{3,7},{8,12},{9,13},{10,14},{11,15},{16,20},{17,... | collective-permute-start | bytes 245768 | tf_op jit(solution)/shard_map/ppermute | solution.py:15
  61.5 2.7 %collective-permute-start.5 = (bf16[2,1,10,10,128]{4,3,2,1,0:T(8,128)(2,1)S(1)}, bf16[2,1,10,10,128]{4,3,2,1,0:T(8,128)(2,1)S(1)}, u32[]{:S(2)}, u32[]{:S(2)}) collective-permute-start(bf16[2,1,10,10,128]{4,3,2,1,0:T(8,128)(2,1)S(1)} %get-tuple-element.28), channel_id=1, source_target_pairs={} | collective-permute-start | bytes 153608 | tf_op jit(solution)/shard_map/ppermute | solution.py:15
  63.5 0.7 collective-permute-start.4
  66.5 6.3 %copy-start.3 = (bf16[2,1,16,8,8,128]{5,4,3,2,1,0:T(8,128)(2,1)S(1)}, bf16[2,1,16,8,8,128]{5,4,3,2,1,0:T(8,128)(2,1)}, u32[]{:S(2)}) copy-start(bf16[2,1,16,8,8,128]{5,4,3,2,1,0:T(8,128)(2,1)} %param.9) | copy-start | bytes 1572868
  86.1 106.9 %all-reduce.2.cloned.1.call-start = ((), (), s32[]{:S(2)}) async-start(), calls=%async_computation.2 | async-start | bytes 442368 | tf_op jit(solution)/shard_map/psum | solution.py:105
  86.3 6.9 %collective-permute-start.7 = (bf16[2,16,8,1,128]{4,3,2,1,0:T(2,128)(2,1)S(1)}, bf16[2,16,8,1,128]{4,3,2,1,0:T(2,128)(2,1)S(1)}, u32[]{:S(2)}, u32[]{:S(2)}) collective-permute-start(bf16[2,16,8,1,128]{4,3,2,1,0:T(2,128)(2,1)S(1)} %get-tuple-element.36), channel_id=1, source_target_pairs={{1,0},{2,1},{3,2},{4,3},{5,4},{6,5},{7,6},{9,8},{10,9},{11,10},{12... | collective-permute-start | bytes 196616 | tf_op jit(solution)/shard_map/ppermute | solution.py:15
  87.6 7.1 %collective-permute-start.6 = (bf16[2,16,8,1,128]{4,3,2,1,0:T(2,128)(2,1)S(1)}, bf16[2,16,8,1,128]{4,3,2,1,0:T(2,128)(2,1)S(1)}, u32[]{:S(2)}, u32[]{:S(2)}) collective-permute-start(bf16[2,16,8,1,128]{4,3,2,1,0:T(2,128)(2,1)S(1)} %get-tuple-element.35), channel_id=1, source_target_pairs={{0,1},{1,2},{2,3},{3,4},{4,5},{5,6},{6,7},{8,9},{9,10},{10,11},{11... | collective-permute-start | bytes 196616 | tf_op jit(solution)/shard_map/ppermute | solution.py:15
  95.0 22.5 %collective-permute-start.9 = (bf16[2,16,1,10,128]{4,3,2,1,0:T(8,128)(2,1)S(1)}, bf16[2,16,1,10,128]{4,3,2,1,0:T(8,128)(2,1)S(1)}, u32[]{:S(2)}, u32[]{:S(2)}) collective-permute-start(bf16[2,16,1,10,128]{4,3,2,1,0:T(8,128)(2,1)S(1)} %get-tuple-element.32), channel_id=1, source_target_pairs={{4,0},{5,1},{6,2},{7,3},{12,8},{13,9},{14,10},{15,11},{20,16},{21,... | collective-permute-start | bytes 245768 | tf_op jit(solution)/shard_map/ppermute | solution.py:15
  96.3 21.5 %collective-permute-start.8 = (bf16[2,16,1,10,128]{4,3,2,1,0:T(8,128)(2,1)S(1)}, bf16[2,16,1,10,128]{4,3,2,1,0:T(8,128)(2,1)S(1)}, u32[]{:S(2)}, u32[]{:S(2)}) collective-permute-start(bf16[2,16,1,10,128]{4,3,2,1,0:T(8,128)(2,1)S(1)} %get-tuple-element.31), channel_id=1, source_target_pairs={{0,4},{1,5},{2,6},{3,7},{8,12},{9,13},{10,14},{11,15},{16,20},{17,... | collective-permute-start | bytes 245768 | tf_op jit(solution)/shard_map/ppermute | solution.py:15
  117.9 1.6 collective-permute-start.11
  118.5 0.9 collective-permute-start.10
  159.9 33.1 %copy-start.1 = (f32[432,128]{1,0:T(8,128)S(1)}, f32[432,128]{1,0:T(8,128)}, u32[]{:S(2)}) copy-start(f32[432,128]{1,0:T(8,128)} %param.6) | copy-start | bytes 663556
  159.9 33.1 %copy-start.4 = (f32[432,128]{1,0:T(8,128)S(1)}, f32[432,128]{1,0:T(8,128)}, u32[]{:S(2)}) copy-start(f32[432,128]{1,0:T(8,128)} %param.7) | copy-start | bytes 663556
  159.9 33.1 %copy-start.5 = (f32[432,128]{1,0:T(8,128)S(1)}, f32[432,128]{1,0:T(8,128)}, u32[]{:S(2)}) copy-start(f32[432,128]{1,0:T(8,128)} %param.8) | copy-start | bytes 663556
Sparse Core Ops, SparseCore 0:
  86.2 73.5 reduce-scatter.1
  162.2 30.7 all-reduce.1
where the time goes:
time: 204 us; the launch traced here: 203 us
  waiting for transfers between devices  76.2 us (37%)
  starting transfers between devices  37.5 us (18%)
  blocking collectives  35.9 us (18%)
  matrix products  23.6 us (12%)
  between operations  14.5 us (7%)
  other arithmetic  11.4 us (6%)
  local copies, waits for them, and re-layouts  4.21 us (2%)
    reduce_scatter x1, waiting for transfers between devices, local(): lax.psum_scatter(local_terms, 'space', scatter_dimension=0, tiled=True)  39.6 us
    ppermute x12, starting transfers between devices, shifted(): return lax.ppermute(value, axis, pairs)  37.4 us
    all_gather x1, blocking collectives, local(): whole = lax.all_gather(rows_bf, 'space', axis=0, tiled=True)  35.9 us
    psum x1, waiting for transfers between devices, local(): weight_grad = lax.psum(owned, 'sample')  24.8 us
    conv_general_dilated x2, matrix products, convolve(): lax.conv_general_dilated(field, kernel, (1, 1, 1), 'VALID', dimension_num...  13.5 us
    ppermute x12, waiting for transfers between devices, shifted(): return lax.ppermute(value, axis, pairs)  11.7 us
    dot_general x27, matrix products, kernel_terms(): lax.dot_general(window, grad_pre, (((0, 1, 2, 3), (0, 1, 2, 3)), ((), ())...  10.1 us
    concatenate x4, other arithmetic, extend(): field = jnp.concatenate([below, field, above], dim)  4.4 us
  transfers between devices with their start and end apart: 14, of which 9 were waited for; matrix products, arithmetic and copies ran while one was open for 6% of the time, Pallas kernels for 0%

commit v1 on v0

--- a/solution.py
+++ b/solution.py
@@ -102,7 +102,7 @@
     )
     local_terms = kernel_terms(padded, grad_pre) * float(total) ** (-0.5)
     owned = lax.psum_scatter(local_terms, "space", scatter_dimension=0, tiled=True)
-    weight_grad = lax.psum(owned, "sample")
+    weight_grad = lax.all_gather(owned, "sample").sum(axis=0)
     new_moment = 0.9 * moment + 0.1 * weight_grad
     new_second = 0.999 * second + 0.001 * weight_grad * weight_grad
     first_fix = 1.0 - 0.9**10

time: 204 us -> 178 us (0.87)
  waiting for transfers between devices: 76.2 us -> 44.3 us
  blocking collectives: 35.9 us -> 45.3 us
    psum x1 -> x0, waiting for transfers between devices: 24.8 us -> none  [local(): weight_grad = lax.psum(owned, 'sample')]
    all_gather x0 -> x1, blocking collectives: none -> 9.32 us  [local(): weight_grad = lax.all_gather(owned, 'sample').sum(axis=0)]
    reduce_scatter x1, waiting for transfers between devices: 39.6 us -> 32.3 us  [local(): lax.psum_scatter(local_terms, 'space', scatter_dimension=0, tiled=True)]
  transfers between devices with their start and end apart: 14 -> 13, of which waited for: 9 -> 8; matrix products, arithmetic and copies ran while one was open for 6% -> 6% of each run, Pallas kernels for 0% -> 0%
where the time goes in v1:
time: 178 us; the launch traced here: 177 us
  blocking collectives  45.3 us (25%)
  waiting for transfers between devices  44.3 us (25%)
  starting transfers between devices  37.4 us (21%)
  matrix products  22.5 us (13%)
  between operations  14.5 us (8%)
  other arithmetic  10.5 us (6%)
  local copies, waits for them, and re-layouts  2.64 us (1%)
    ppermute x12, starting transfers between devices, shifted(): return lax.ppermute(value, axis, pairs)  37.4 us
    all_gather x1, blocking collectives, local(): whole = lax.all_gather(rows_bf, 'space', axis=0, tiled=True)  35.9 us
    reduce_scatter x1, waiting for transfers between devices, local(): lax.psum_scatter(local_terms, 'space', scatter_dimension=0, tiled=True)  32.3 us
    conv_general_dilated x2, matrix products, convolve(): lax.conv_general_dilated(field, kernel, (1, 1, 1), 'VALID', dimension_num...  12.5 us
    ppermute x12, waiting for transfers between devices, shifted(): return lax.ppermute(value, axis, pairs)  12 us
    dot_general x27, matrix products, kernel_terms(): lax.dot_general(window, grad_pre, (((0, 1, 2, 3), (0, 1, 2, 3)), ((), ())...  10.1 us
    all_gather x1, blocking collectives, local(): weight_grad = lax.all_gather(owned, 'sample').sum(axis=0)  9.32 us
    concatenate x4, other arithmetic, extend(): field = jnp.concatenate([below, field, above], dim)  4.4 us
  transfers between devices with their start and end apart: 13, of which 8 were waited for; matrix products, arithmetic and copies ran while one was open for 6% of the time, Pallas kernels for 0%

profile of v1, /device:TPU:0, one launch (start us, length us, event | category | flops | bytes accessed | tf_op | source)
XLA Modules:
  0.0 177.2 jit_solution(913169068227492812)
XLA Ops:
  7.2 1.5 fusion.71
  8.7 1.3 collective-permute-start.1
  10.0 5.5 %collective-permute-start = (bf16[2,16,8,1,128]{4,3,2,1,0:T(2,128)(2,1)S(1)}, bf16[2,16,8,1,128]{4,3,2,1,0:T(2,128)(2,1)S(1)}, u32[]{:S(2)}, u32[]{:S(2)}) collective-permute-start(bf16[2,16,8,1,128]{4,3,2,1,0:T(2,128)(2,1)S(1)} %get-tuple-element.37), channel_id=1, source_target_pairs={{0,1},{1,2},{2,3},{3,4},{4,5},{5,6},{6,7},{8,9},{9,10},{10,11},{11... | collective-permute-start | bytes 196616 | tf_op jit(solution)/shard_map/ppermute | solution.py:15
  15.6 1.0 convert_element_type.18
  16.6 0.6 collective-permute-done.1
  17.3 2.8 %collective-permute-done = bf16[2,16,8,1,128]{4,3,2,1,0:T(2,128)(2,1)S(1)} collective-permute-done((bf16[2,16,8,1,128]{4,3,2,1,0:T(2,128)(2,1)S(1)}, bf16[2,16,8,1,128]{4,3,2,1,0:T(2,128)(2,1)S(1)}, u32[]{:S(2)}, u32[]{:S(2)}) %collective-permute-start) | collective-permute-done | bytes 65568 | tf_op jit(solution)/shard_map/ppermute | solution.py:15
  20.4 1.3 collective-permute-start.3
  21.7 35.9 %all_gather.9 = bf16[3456,128]{1,0:T(8,128)(2,1)S(1)} all-gather(bf16[432,128]{1,0:T(8,128)(2,1)S(1)} %convert_element_type.18), channel_id=1, replica_groups=mesh['sample'=4,'space'=8] {'space'}, dimensions={0}, use_global_device_ids=true | all-gather | bytes 995328 | tf_op jit(solution)/shard_map/all_gather | solution.py:85
  57.6 1.3 collective-permute-start.2
  59.0 2.5 %collective-permute-done.2 = bf16[2,16,1,10,128]{4,3,2,1,0:T(8,128)(2,1)S(1)} collective-permute-done((bf16[2,16,1,10,128]{4,3,2,1,0:T(8,128)(2,1)S(1)}, bf16[2,16,1,10,128]{4,3,2,1,0:T(8,128)(2,1)S(1)}, u32[]{:S(2)}, u32[]{:S(2)}) %collective-permute-start.2) | collective-permute-done | bytes 81952 | tf_op jit(solution)/shard_map/ppermute | solution.py:15
  61.5 0.7 collective-permute-start.5
  62.2 1.4 pad_maximum_fusion.3
  63.6 0.7 collective-permute-start.4
  64.3 0.7 pad_maximum_fusion
  65.0 1.5 pad_maximum_fusion.2
  66.6 6.3 %fusion.36 = f32[2,16,8,8,128]{4,0,3,2,1:T(2,128)S(1)} fusion(bf16[3,3,3,128,128]{4,3,2,1,0:T(8,128)(2,1)S(1)} %bitcast.274, bf16[2,18,10,10,128]{4,3,2,1,0:T(8,128)(2,1)S(1)} %pad_maximum_fusion), kind=kOutput, calls=%fused_computation.73 | convolution fusion | flops 1811939328 | bytes 2854912 | tf_op jit(solution)/shard_map/conv_general_dilated | solution.py:19
  72.9 1.6 fusion.34
  74.8 0.4 fusion.26
  75.2 0.4 fusion.25
  77.0 0.4 fusion.20
  77.4 0.4 fusion.19
  78.2 0.4 fusion.17
  78.5 0.4 fusion.16
  78.9 0.4 fusion.15
  79.7 0.5 fusion.13
  81.7 0.4 fusion.8
  82.1 0.4 fusion.7
  82.8 0.4 fusion.5
  83.2 0.4 fusion.4
  83.9 0.4 fusion.2
  84.3 0.4 fusion.1
  84.7 1.4 broadcast_multiply_fusion
  86.3 1.3 collective-permute-start.7
  87.6 4.6 %collective-permute-start.6 = (bf16[2,16,8,1,128]{4,3,2,1,0:T(2,128)(2,1)S(1)}, bf16[2,16,8,1,128]{4,3,2,1,0:T(2,128)(2,1)S(1)}, u32[]{:S(2)}, u32[]{:S(2)}) collective-permute-start(bf16[2,16,8,1,128]{4,3,2,1,0:T(2,128)(2,1)S(1)} %get-tuple-element.35), channel_id=1, source_target_pairs={{0,1},{1,2},{2,3},{3,4},{4,5},{5,6},{6,7},{8,9},{9,10},{10,11},{11... | collective-permute-start | bytes 196616 | tf_op jit(solution)/shard_map/ppermute | solution.py:15
  92.2 1.0 collective-permute-done.7
  93.3 1.3 collective-permute-done.6
  95.0 1.3 collective-permute-start.9
  96.3 18.0 %collective-permute-start.8 = (bf16[2,16,1,10,128]{4,3,2,1,0:T(8,128)(2,1)S(1)}, bf16[2,16,1,10,128]{4,3,2,1,0:T(8,128)(2,1)S(1)}, u32[]{:S(2)}, u32[]{:S(2)}) collective-permute-start(bf16[2,16,1,10,128]{4,3,2,1,0:T(8,128)(2,1)S(1)} %get-tuple-element.31), channel_id=1, source_target_pairs={{0,4},{1,5},{2,6},{3,7},{8,12},{9,13},{10,14},{11,15},{16,20},{17,... | collective-permute-start | bytes 245768 | tf_op jit(solution)/shard_map/ppermute | solution.py:15
  114.3 3.3 %collective-permute-done.9 = bf16[2,16,1,10,128]{4,3,2,1,0:T(8,128)(2,1)S(1)} collective-permute-done((bf16[2,16,1,10,128]{4,3,2,1,0:T(8,128)(2,1)S(1)}, bf16[2,16,1,10,128]{4,3,2,1,0:T(8,128)(2,1)S(1)}, u32[]{:S(2)}, u32[]{:S(2)}) %collective-permute-start.9) | collective-permute-done | bytes 81952 | tf_op jit(solution)/shard_map/ppermute | solution.py:15
  117.6 0.5 collective-permute-done.8
  118.2 0.7 collective-permute-start.11
  118.8 0.9 collective-permute-start.10
  119.8 0.7 pad_maximum_fusion.1
  120.5 6.2 %fusion = bf16[2,1,16,8,8,128]{5,0,4,3,2,1:T(2,128)(2,1)S(1)} fusion(bf16[3,3,3,128,128]{4,3,2,1,0:T(8,128)(2,1)S(1)} %bitcast.275, bf16[2,18,10,10,128]{4,3,2,1,0:T(8,128)(2,1)S(1)} %pad_maximum_fusion.1), kind=kOutput, calls=%fused_computation.7 | convolution fusion | flops 1812201472 | bytes 2330624 | tf_op jit(solution)/shard_map/conv_general_dilated | solution.py:19
  126.8 0.9 copy.134
  127.7 32.3 %reduce-scatter.2.cloned.1.call-done = f32[432,128]{1,0:T(8,128)} async-done(((f32[3456,128]{1,0:T(8,128)}), f32[432,128]{1,0:T(8,128)}) %reduce-scatter.2.cloned.1.call-update) | async-done | bytes 221200 | tf_op jit(solution)/shard_map/reduce_scatter | solution.py:104
  160.0 9.3 %all-gather = f32[1728,128]{1,0:T(8,128)S(1)} all-gather(f32[432,128]{1,0:T(8,128)} %reduce-scatter.2.cloned.1.call-done), channel_id=2, replica_groups=mesh['sample'=4,'space'=8] {'sample'}, dimensions={0}, use_global_device_ids=true | all-gather | bytes 1105920 | tf_op jit(solution)/shard_map/all_gather | solution.py:105
  169.4 0.9 divide_subtract_fusion
  (50 shorter events, 6.1 us)
Async XLA Ops:
  7.2 13.1 %copy-start = (bf16[2,1,16,8,8,128]{5,4,3,2,1,0:T(8,128)(2,1)S(1)}, bf16[2,1,16,8,8,128]{5,4,3,2,1,0:T(8,128)(2,1)}, u32[]{:S(2)}) copy-start(bf16[2,1,16,8,8,128]{5,4,3,2,1,0:T(8,128)(2,1)} %param.5) | copy-start | bytes 1572868
  7.2 152.8 %reduce-scatter.2.cloned.1.call-start = ((), (), s32[]{:S(2)}) async-start(), calls=%async_computation.1 | async-start | bytes 1990656 | tf_op jit(solution)/shard_map/reduce_scatter | solution.py:104
  8.7 8.4 %collective-permute-start.1 = (bf16[2,16,8,1,128]{4,3,2,1,0:T(2,128)(2,1)S(1)}, bf16[2,16,8,1,128]{4,3,2,1,0:T(2,128)(2,1)S(1)}, u32[]{:S(2)}, u32[]{:S(2)}) collective-permute-start(bf16[2,16,8,1,128]{4,3,2,1,0:T(2,128)(2,1)S(1)} %get-tuple-element.38), channel_id=1, source_target_pairs={{1,0},{2,1},{3,2},{4,3},{5,4},{6,5},{7,6},{9,8},{10,9},{11,10},{12... | collective-permute-start | bytes 196616 | tf_op jit(solution)/shard_map/ppermute | solution.py:15
  10.0 10.1 %collective-permute-start = (bf16[2,16,8,1,128]{4,3,2,1,0:T(2,128)(2,1)S(1)}, bf16[2,16,8,1,128]{4,3,2,1,0:T(2,128)(2,1)S(1)}, u32[]{:S(2)}, u32[]{:S(2)}) collective-permute-start(bf16[2,16,8,1,128]{4,3,2,1,0:T(2,128)(2,1)S(1)} %get-tuple-element.37), channel_id=1, source_target_pairs={{0,1},{1,2},{2,3},{3,4},{4,5},{5,6},{6,7},{8,9},{9,10},{10,11},{11... | collective-permute-start | bytes 196616 | tf_op jit(solution)/shard_map/ppermute | solution.py:15
  20.4 38.5 %collective-permute-start.3 = (bf16[2,16,1,10,128]{4,3,2,1,0:T(8,128)(2,1)S(1)}, bf16[2,16,1,10,128]{4,3,2,1,0:T(8,128)(2,1)S(1)}, u32[]{:S(2)}, u32[]{:S(2)}) collective-permute-start(bf16[2,16,1,10,128]{4,3,2,1,0:T(8,128)(2,1)S(1)} %get-tuple-element.34), channel_id=1, source_target_pairs={{4,0},{5,1},{6,2},{7,3},{12,8},{13,9},{14,10},{15,11},{20,16},{21,... | collective-permute-start | bytes 245768 | tf_op jit(solution)/shard_map/ppermute | solution.py:15
  57.6 3.8 %collective-permute-start.2 = (bf16[2,16,1,10,128]{4,3,2,1,0:T(8,128)(2,1)S(1)}, bf16[2,16,1,10,128]{4,3,2,1,0:T(8,128)(2,1)S(1)}, u32[]{:S(2)}, u32[]{:S(2)}) collective-permute-start(bf16[2,16,1,10,128]{4,3,2,1,0:T(8,128)(2,1)S(1)} %get-tuple-element.33), channel_id=1, source_target_pairs={{0,4},{1,5},{2,6},{3,7},{8,12},{9,13},{10,14},{11,15},{16,20},{17,... | collective-permute-start | bytes 245768 | tf_op jit(solution)/shard_map/ppermute | solution.py:15
  61.5 2.7 %collective-permute-start.5 = (bf16[2,1,10,10,128]{4,3,2,1,0:T(8,128)(2,1)S(1)}, bf16[2,1,10,10,128]{4,3,2,1,0:T(8,128)(2,1)S(1)}, u32[]{:S(2)}, u32[]{:S(2)}) collective-permute-start(bf16[2,1,10,10,128]{4,3,2,1,0:T(8,128)(2,1)S(1)} %get-tuple-element.28), channel_id=1, source_target_pairs={} | collective-permute-start | bytes 153608 | tf_op jit(solution)/shard_map/ppermute | solution.py:15
  63.6 0.7 collective-permute-start.4
  66.6 6.3 %copy-start.3 = (bf16[2,1,16,8,8,128]{5,4,3,2,1,0:T(8,128)(2,1)S(1)}, bf16[2,1,16,8,8,128]{5,4,3,2,1,0:T(8,128)(2,1)}, u32[]{:S(2)}) copy-start(bf16[2,1,16,8,8,128]{5,4,3,2,1,0:T(8,128)(2,1)} %param.9) | copy-start | bytes 1572868
  86.3 6.9 %collective-permute-start.7 = (bf16[2,16,8,1,128]{4,3,2,1,0:T(2,128)(2,1)S(1)}, bf16[2,16,8,1,128]{4,3,2,1,0:T(2,128)(2,1)S(1)}, u32[]{:S(2)}, u32[]{:S(2)}) collective-permute-start(bf16[2,16,8,1,128]{4,3,2,1,0:T(2,128)(2,1)S(1)} %get-tuple-element.36), channel_id=1, source_target_pairs={{1,0},{2,1},{3,2},{4,3},{5,4},{6,5},{7,6},{9,8},{10,9},{11,10},{12... | collective-permute-start | bytes 196616 | tf_op jit(solution)/shard_map/ppermute | solution.py:15
  87.6 7.1 %collective-permute-start.6 = (bf16[2,16,8,1,128]{4,3,2,1,0:T(2,128)(2,1)S(1)}, bf16[2,16,8,1,128]{4,3,2,1,0:T(2,128)(2,1)S(1)}, u32[]{:S(2)}, u32[]{:S(2)}) collective-permute-start(bf16[2,16,8,1,128]{4,3,2,1,0:T(2,128)(2,1)S(1)} %get-tuple-element.35), channel_id=1, source_target_pairs={{0,1},{1,2},{2,3},{3,4},{4,5},{5,6},{6,7},{8,9},{9,10},{10,11},{11... | collective-permute-start | bytes 196616 | tf_op jit(solution)/shard_map/ppermute | solution.py:15
  95.0 22.6 %collective-permute-start.9 = (bf16[2,16,1,10,128]{4,3,2,1,0:T(8,128)(2,1)S(1)}, bf16[2,16,1,10,128]{4,3,2,1,0:T(8,128)(2,1)S(1)}, u32[]{:S(2)}, u32[]{:S(2)}) collective-permute-start(bf16[2,16,1,10,128]{4,3,2,1,0:T(8,128)(2,1)S(1)} %get-tuple-element.32), channel_id=1, source_target_pairs={{4,0},{5,1},{6,2},{7,3},{12,8},{13,9},{14,10},{15,11},{20,16},{21,... | collective-permute-start | bytes 245768 | tf_op jit(solution)/shard_map/ppermute | solution.py:15
  96.3 21.8 %collective-permute-start.8 = (bf16[2,16,1,10,128]{4,3,2,1,0:T(8,128)(2,1)S(1)}, bf16[2,16,1,10,128]{4,3,2,1,0:T(8,128)(2,1)S(1)}, u32[]{:S(2)}, u32[]{:S(2)}) collective-permute-start(bf16[2,16,1,10,128]{4,3,2,1,0:T(8,128)(2,1)S(1)} %get-tuple-element.31), channel_id=1, source_target_pairs={{0,4},{1,5},{2,6},{3,7},{8,12},{9,13},{10,14},{11,15},{16,20},{17,... | collective-permute-start | bytes 245768 | tf_op jit(solution)/shard_map/ppermute | solution.py:15
  118.2 1.6 collective-permute-start.11
  118.8 0.9 collective-permute-start.10
  126.7 42.7 %copy-start.1 = (f32[432,128]{1,0:T(8,128)S(1)}, f32[432,128]{1,0:T(8,128)}, u32[]{:S(2)}) copy-start(f32[432,128]{1,0:T(8,128)} %param.6) | copy-start | bytes 663556
  126.7 42.7 %copy-start.4 = (f32[432,128]{1,0:T(8,128)S(1)}, f32[432,128]{1,0:T(8,128)}, u32[]{:S(2)}) copy-start(f32[432,128]{1,0:T(8,128)} %param.7) | copy-start | bytes 663556
  126.7 42.7 %copy-start.5 = (f32[432,128]{1,0:T(8,128)S(1)}, f32[432,128]{1,0:T(8,128)}, u32[]{:S(2)}) copy-start(f32[432,128]{1,0:T(8,128)} %param.8) | copy-start | bytes 663556
  169.4 0.9 copy-start.2
Sparse Core Ops, SparseCore 0:
  86.3 73.6 reduce-scatter.1
